TPU v7x, 128 devices: a whole 4x4x4 slice. The times are simulated.
128 devices in a mesh: tm: 32 (over z, y, core), chan: 4 (over x).
Axes of the slice: x: 4, y: 4, z: 4, core: 2. Of those that a mesh axis runs over, the one named last changes fastest.
Arguments:
- coarse: bfloat16 [2, 98304, 4096], P(None, 'tm', 'chan'), may hold values from -6 to 6
- prototype: float32 [16, 1024], replicated, may hold values from -4 to 4
- req_block: int32 [4, 4], replicated, may hold values from 0 to 31, as said below
- req_start: int32 [4, 4], replicated, may hold values from 0 to 80, as said below
- req_frames: int32 [4, 4], replicated, may hold values from 1 to 81
- req_count: int32 [4], replicated, may hold values from 1 to 4, as said below
Outputs:
- spectra: bfloat16 [96, 4, 4, 2, 1024, 128], P('tm', 'chan')
Inputs may be any that keep to these rules, and one draw needn't show every extreme that they name: `req_block`: among the live slots of one owner at most 2 name blocks b with the same b // 8; in every draw some owner reaches 2. req_start + req_frames <= 81 in every slot; in every draw some live slot starts at hop 81 - 1 and some live slot spans all 81 frames. Slots q < req_count[c] of owner c are live, the others are empty; in every draw some owner has 4 live slots.
All inputs are finite; a program needn't handle non-finite values.
Results may differ from a plain program's by a relative error of at most 0.001.
Values may be sent and summed in bfloat16 or wider, within the bound.
No kernel may reach another device: no remote copies, remote signals or barrier semaphores. Data moves between devices by JAX's collectives and lax.ppermute only.
A program may use at most 256 MiB of HBM per device.

v0:
```python
import math
import jax
import jax.numpy as jnp
from jax import lax
from jax.sharding import PartitionSpec as P

BLOCKW = 128
NFINE = 1024
TAPS = 16
HOPS_DEV = 3
MAXREQ = 4
PAIR = 2


def build_table():
    index_line = jnp.arange(NFINE, dtype=jnp.int32)
    products = index_line[:, None] * index_line[None, :] % NFINE
    angles = products.astype(jnp.float32) * (2.0 * math.pi / NFINE)
    cosine = jnp.cos(angles) / math.sqrt(NFINE)
    sine = jnp.sin(angles) / math.sqrt(NFINE)
    upper = jnp.concatenate([cosine, sine], axis=1)
    lower = jnp.concatenate([-sine, cosine], axis=1)
    return jnp.concatenate([upper, lower], axis=0)


def shards(coarse, prototype, req_block, req_start, req_frames, req_count):
    owners = lax.axis_size("chan")
    column = lax.axis_index("chan")
    row_index = lax.axis_index("tm")
    time_devices = lax.axis_size("tm")
    per_column = coarse.shape[2] // BLOCKW
    coarse_data = coarse.reshape(2, HOPS_DEV, NFINE, per_column, BLOCKW)
    slot_ids = jnp.arange(MAXREQ, dtype=jnp.int32)
    is_live = slot_ids[None, :] < req_count[:, None]
    sources = req_block // per_column
    is_mine = is_live & (sources == column)
    ranking = jnp.cumsum(is_mine.astype(jnp.int32), axis=1) - 1
    pair_ids = jnp.arange(PAIR, dtype=jnp.int32)
    picked = is_mine[:, None, :] & (ranking[:, None, :] == pair_ids[None, :, None])
    local_ids = req_block - column * per_column
    block_ids = jnp.arange(per_column, dtype=jnp.int32)
    matches = picked[:, :, :, None] & (
        local_ids[:, None, :, None] == block_ids[None, None, None, :]
    )
    chooser = jnp.any(matches, axis=2).astype(jnp.bfloat16)
    outgoing = jnp.einsum(
        "dpb,xhkbc->dpxhkc", chooser, coarse_data, preferred_element_type=jnp.float32
    ).astype(jnp.bfloat16)
    incoming = lax.all_to_all(outgoing, "chan", split_axis=0, concat_axis=0, tiled=True)
    owner_ids = jnp.arange(owners, dtype=jnp.int32)
    row_pick = owner_ids == column
    my_block = jnp.sum(jnp.where(row_pick[:, None], req_block, 0), axis=0)
    my_start = jnp.sum(jnp.where(row_pick[:, None], req_start, 0), axis=0)
    my_frames = jnp.sum(jnp.where(row_pick[:, None], req_frames, 0), axis=0)
    my_count = jnp.sum(jnp.where(row_pick, req_count, 0))
    my_live = slot_ids < my_count
    my_source = my_block // per_column
    earlier = (
        my_live[:, None]
        & my_live[None, :]
        & (my_source[:, None] == my_source[None, :])
        & (slot_ids[None, :] < slot_ids[:, None])
    )
    my_rank = jnp.sum(earlier.astype(jnp.int32), axis=1)
    arrival = my_source * PAIR + my_rank
    taker = (
        my_live[:, None] & (arrival[:, None] == jnp.arange(owners * PAIR, dtype=jnp.int32)[None, :])
    ).astype(jnp.bfloat16)
    arrived = incoming.reshape(owners * PAIR, 2, HOPS_DEV, NFINE, BLOCKW)
    slots = jnp.einsum(
        "qs,sxhkc->qxhkc", taker, arrived, preferred_element_type=jnp.float32
    ).astype(jnp.bfloat16)
    hop_ids = row_index * HOPS_DEV + jnp.arange(HOPS_DEV, dtype=jnp.int32)
    active = (
        my_live[:, None]
        & (hop_ids[None, :] >= my_start[:, None])
        & (hop_ids[None, :] < (my_start + my_frames)[:, None])
    )
    table = build_table()
    widest = MAXREQ * BLOCKW
    share = widest // time_devices
    all_hops = HOPS_DEV * time_devices
    sending = slots.transpose(2, 1, 3, 0, 4).reshape(HOPS_DEV, 2, NFINE, widest)
    gathered_cols = lax.all_to_all(sending, "tm", split_axis=3, concat_axis=0, tiled=True)
    padding = jnp.zeros((TAPS - 1, 2, NFINE, share), jnp.bfloat16)
    extended = jnp.concatenate([gathered_cols, padding], axis=0)
    col_filtered = jnp.zeros((all_hops, 2, NFINE, share), jnp.float32)
    for tap_index in range(TAPS):
        weights = prototype[tap_index][None, None, :, None]
        col_filtered = col_filtered + weights * extended[tap_index : tap_index + all_hops].astype(
            jnp.float32
        )
    flat = col_filtered.transpose(1, 2, 0, 3).reshape(2 * NFINE, all_hops * share)
    result = jnp.dot(
        table, flat, precision=lax.Precision.HIGHEST, preferred_element_type=jnp.float32
    )
    result = result.reshape(2, NFINE, all_hops, share).transpose(2, 0, 1, 3).astype(jnp.bfloat16)
    returned = lax.all_to_all(result, "tm", split_axis=0, concat_axis=3, tiled=True)
    spectra = returned.reshape(HOPS_DEV, 2, NFINE, MAXREQ, BLOCKW).transpose(0, 3, 1, 2, 4)
    keep = active.T[:, :, None, None, None]
    spectra = jnp.where(keep, spectra, jnp.zeros_like(spectra))
    return spectra[:, None]


def solution(mesh):
    return jax.shard_map(
        shards,
        mesh=mesh,
        in_specs=(P(None, "tm", "chan"), P(), P(), P(), P(), P()),
        out_specs=P("tm", "chan", None, None, None, None),
        check_vma=False,
    )
```

profile of v0, /device:TPU:0, one launch (start us, length us, event | category | flops | bytes accessed | tf_op | source)
XLA Modules:
  0.0 602.9 jit_solution(15410880582212164777)
XLA Ops:
  0.0 0.8 select_reduce_fusion.1
  0.9 0.8 fusion.28
  1.6 0.2 reduce_window_sum.11
  1.8 7.8 %copy.43 = bf16[768,8,8,128]{3,2,1,0:T(8,128)(2,1)S(1)} copy(bf16[768,8,8,128]{3,1,2,0:T(8,128)(2,1)} %bitcast.79) | data formatting | bytes 25165824
  9.6 0.1 and_reduce_fusion
  9.7 6.6 %convolution_convert_fusion = bf16[4,2,2,3,1024,128]{5,0,4,3,2,1:T(4,128)(2,1)} fusion(bf16[2,3,1024,8,128,1]{4,3,2,1,0,5:T(8,128)(2,1)S(1)} %bitcast.72, pred[4,2,8,1,1,1]{2,1,0,5,4,3:T(4,128)(4,1)S(1)} %bitcast.97), kind=kOutput, calls=%fused_computation.7 | convolution fusion | flops 106954752 | bytes 25165888 | tf_op jit(solution)/shard_map/dpb,xhkbc->dpxhkc/dot_general | solution.py:46
  16.3 11.6 %copy.27 = bf16[4,2,2,3,1024,128]{5,4,3,2,1,0:T(8,128)(2,1)} copy(bf16[4,2,2,3,1024,128]{5,0,4,3,2,1:T(4,128)(2,1)} %convolution_convert_fusion) | data formatting | bytes 25165824 | tf_op jit(solution)/shard_map/convert_element_type | solution.py:48
  27.9 6.5 %all-to-all-start = ((bf16[4,2,2,3,1024,128]{5,4,3,2,1,0:T(8,128)(2,1)}), bf16[4,2,2,3,1024,128]{5,4,3,2,1,0:T(8,128)(2,1)}, u32[]{:S(2)}, u32[]{:S(2)}) async-start(bf16[4,2,2,3,1024,128]{5,4,3,2,1,0:T(8,128)(2,1)} %copy.27), calls=%async_computation | async-start | bytes 25165824 | tf_op jit(solution)/shard_map/all_to_all | solution.py:49
  34.4 0.6 select_reduce_fusion.3
  35.0 0.6 iota_compare_fusion.5
  35.7 0.2 convert_reduce_fusion
  35.9 137.4 %all-to-all-done = bf16[4,2,2,3,1024,128]{5,4,3,2,1,0:T(8,128)(2,1)} async-done(((bf16[4,2,2,3,1024,128]{5,4,3,2,1,0:T(8,128)(2,1)}), bf16[4,2,2,3,1024,128]{5,4,3,2,1,0:T(8,128)(2,1)}, u32[]{:S(2)}, u32[]{:S(2)}) %all-to-all-start) | async-done | bytes 12582944 | tf_op jit(solution)/shard_map/all_to_all | solution.py:49
  173.3 14.5 %convert_bitcast_fusion.1 = bf16[3,2,1024,4,128]{4,3,2,0,1:T(4,128)(2,1)} fusion(bf16[8,2,3,1024,128]{4,3,2,1,0:T(8,128)(2,1)} %bitcast.7, s32[4]{0:T(128)S(1)} %multiply_add_fusion, pred[4]{0:T(512)(128)(4,1)S(1)} %iota_compare_fusion.5), kind=kOutput, calls=%fused_computation.22 | convolution fusion | flops 53477440 | bytes 18874388 | tf_op jit(solution)/shard_map/qs,sxhkc->qxhkc/dot_general | solution.py:70
  187.8 17.6 %copy.42 = bf16[3,2,1024,4,128]{2,1,0,4,3:T(2,128)(2,1)} copy(bf16[3,2,1024,4,128]{4,3,2,0,1:T(4,128)(2,1)} %convert_bitcast_fusion.1) | data formatting | bytes 12582912 | tf_op jit(solution)/shard_map/reshape | solution.py:83
  205.4 9.1 %all-to-all-start.1 = ((bf16[3,2,1024,512]{2,1,0,3:T(2,128)(2,1)}), bf16[3,2,1024,512]{2,1,0,3:T(2,128)(2,1)}, u32[]{:S(2)}, u32[]{:S(2)}) async-start(bf16[3,2,1024,512]{2,1,0,3:T(2,128)(2,1)} %bitcast.74), calls=%async_computation.1 | async-start | bytes 12582912 | tf_op jit(solution)/shard_map/all_to_all | solution.py:84
  214.6 15.5 %fusion.16 = f32[1024,1024]{1,0:T(8,128)S(1)} fusion(), kind=kLoop, calls=%fused_computation.34 | loop fusion | flops 16777216 | bytes 4194304 | tf_op jit(solution)/shard_map/neg | solution.py:22
  230.1 16.6 %sine_multiply_fusion = (f32[1024,1024]{1,0:T(8,128)S(1)}, f32[1024,1024]{1,0:T(8,128)S(1)}) fusion(), kind=kLoop, calls=%fused_computation.29 | loop fusion | flops 16777216 | bytes 8388608 | tf_op jit(solution)/shard_map/div | solution.py:20
  246.7 15.5 %maximum_maximum_fusion = f32[2048,2048]{1,0:T(8,128)} fusion(f32[1024,1024]{1,0:T(8,128)S(1)} %get-tuple-element.28, f32[1024,1024]{1,0:T(8,128)S(1)} %fusion.16, f32[1024,1024]{1,0:T(8,128)S(1)} %get-tuple-element.27), kind=kLoop, calls=%fused_computation | loop fusion | flops 12582912 | bytes 29360128 | tf_op jit(solution)/shard_map/concatenate | solution.py:23
  262.3 29.7 %all-to-all-done.1 = bf16[3,2,1024,512]{2,1,0,3:T(2,128)(2,1)} async-done(((bf16[3,2,1024,512]{2,1,0,3:T(2,128)(2,1)}), bf16[3,2,1024,512]{2,1,0,3:T(2,128)(2,1)}, u32[]{:S(2)}, u32[]{:S(2)}) %all-to-all-start.1) | async-done | bytes 6291488 | tf_op jit(solution)/shard_map/all_to_all | solution.py:84
  291.9 4.8 copy.30
  296.7 3.4 copy.31
  300.1 48.5 %add_bitcast_fusion = f32[2,1024,96,16]{1,3,0,2:T(8,128)} fusion(bf16[96,2,1024,16]{2,3,1,0:T(8,128)(2,1)} %bitcast.77, f32[1024]{0:T(1024)S(1)} %bitcast.95, f32[1024]{0:T(1024)S(1)} %bitcast.96, f32[1024]{0:T(1024)S(1)} %bitcast.82, f32[1024]{0:T(1024)S(1)} %bitcast.83, f32[1024]{0:T(1024)S(1)} %bitcast.84, f32[1024]{0:T(1024)S(1)} %bitcast.85, ...), kind=kLoop, calls=%fused_computation.6 | loop fusion | flops 147849216 | bytes 18939904 | tf_op jit(solution)/shard_map/transpose | solution.py:93
  348.7 22.3 %copy.32 = f32[2,1024,96,16]{1,0,3,2:T(2,128)} copy(f32[2,1024,96,16]{1,3,0,2:T(8,128)} %add_bitcast_fusion) | data formatting | bytes 25165824 | tf_op jit(solution)/shard_map/transpose | solution.py:93
  371.0 15.3 %copy.44 = f32[192,8,2,1024]{3,1,2,0:T(8,128)} copy(f32[192,8,2,1024]{3,2,1,0:T(2,128)} %bitcast.73) | data formatting | bytes 25165824
  386.3 112.1 %convert_bitcast_fusion = bf16[96,2,1024,16]{2,0,3,1:T(8,128)(2,1)S(1)} fusion(f32[2,1024,2048,1]{2,1,3,0:T(8,128)} %bitcast.78, f32[96,16,2048]{2,1,0:T(8,128)} %bitcast.80), kind=kOutput, calls=%fused_computation.10 | convolution fusion | flops 77312557056 | bytes 35651584 | tf_op jit(solution)/shard_map/dot_general | solution.py:94
  498.4 6.2 %copy.34 = bf16[96,2,1024,16]{2,3,1,0:T(8,128)(2,1)} copy(bf16[96,2,1024,16]{2,0,3,1:T(8,128)(2,1)S(1)} %convert_bitcast_fusion) | data formatting | bytes 12582912 | tf_op jit(solution)/shard_map/convert_element_type | solution.py:97
  504.6 4.9 all-to-all-start.2
  509.6 0.1 compare_and_fusion.1
  509.7 77.8 %all-to-all-done.2 = bf16[96,2,1024,16]{2,3,1,0:T(8,128)(2,1)} async-done(((bf16[96,2,1024,16]{2,3,1,0:T(8,128)(2,1)}), bf16[96,2,1024,16]{2,3,1,0:T(8,128)(2,1)}, u32[]{:S(2)}, u32[]{:S(2)}) %all-to-all-start.2) | async-done | bytes 6291488 | tf_op jit(solution)/shard_map/all_to_all | solution.py:98
  587.5 3.5 copy.35
  591.0 3.1 fusion.5
  594.1 8.6 %copy.36 = bf16[3,1,4,2,1024,128]{5,4,3,2,1,0:T(8,128)(2,1)} copy(bf16[3,1,4,2,1024,128]{4,5,2,3,0,1:T(8,128)(2,1)} %fusion.5) | data formatting | bytes 12582912 | tf_op jit(solution)/shard_map/broadcast_in_dim | solution.py:102
  (13 shorter events, 0.2 us)
Async XLA Ops:
  27.9 6.5 %copy-start.1 = (s32[4]{0:T(128)S(1)}, s32[4]{0:T(128)}, u32[]{:S(2)}) copy-start(s32[4]{0:T(128)} %param.11) | copy-start | bytes 52
  27.9 145.4 %all-to-all-start = ((bf16[4,2,2,3,1024,128]{5,4,3,2,1,0:T(8,128)(2,1)}), bf16[4,2,2,3,1024,128]{5,4,3,2,1,0:T(8,128)(2,1)}, u32[]{:S(2)}, u32[]{:S(2)}) async-start(bf16[4,2,2,3,1024,128]{5,4,3,2,1,0:T(8,128)(2,1)} %copy.27), calls=%async_computation | async-start | bytes 25165824 | tf_op jit(solution)/shard_map/all_to_all | solution.py:49
  187.8 26.8 %copy-start = (f32[16,1024]{1,0:T(8,128)S(1)}, f32[16,1024]{1,0:T(8,128)}, u32[]{:S(2)}) copy-start(f32[16,1024]{1,0:T(8,128)} %param.7) | copy-start | bytes 196612
  205.4 86.5 %all-to-all-start.1 = ((bf16[3,2,1024,512]{2,1,0,3:T(2,128)(2,1)}), bf16[3,2,1024,512]{2,1,0,3:T(2,128)(2,1)}, u32[]{:S(2)}, u32[]{:S(2)}) async-start(bf16[3,2,1024,512]{2,1,0,3:T(2,128)(2,1)} %bitcast.74), calls=%async_computation.1 | async-start | bytes 12582912 | tf_op jit(solution)/shard_map/all_to_all | solution.py:84
  504.6 82.8 %all-to-all-start.2 = ((bf16[96,2,1024,16]{2,3,1,0:T(8,128)(2,1)}), bf16[96,2,1024,16]{2,3,1,0:T(8,128)(2,1)}, u32[]{:S(2)}, u32[]{:S(2)}) async-start(bf16[96,2,1024,16]{2,3,1,0:T(8,128)(2,1)} %copy.34), calls=%async_computation.2 | async-start | bytes 12582912 | tf_op jit(solution)/shard_map/all_to_all | solution.py:98
where the time goes:
time: 611 us; the launch traced here: 603 us
  waiting for transfers between devices  245 us (40%)
  matrix products  133 us (22%)
  other arithmetic  103 us (17%)
  local copies, waits for them, and re-layouts  101 us (17%)
  starting transfers between devices  20.5 us (3%)
    all_to_all x1, waiting for transfers between devices, shards(): lax.all_to_all(outgoing, 'chan', split_axis=0, concat_axis=0, tiled=True)  137 us
    dot_general x1, matrix products, shards(): jnp.dot(table, flat, precision=lax.Precision.HIGHEST, preferred_element_t...  112 us
    all_to_all x1, waiting for transfers between devices, shards(): lax.all_to_all(result, 'tm', split_axis=0, concat_axis=3, tiled=True)  77.8 us
    transpose x1, other arithmetic, shards(): col_filtered.transpose(1, 2, 0, 3).reshape(2 * NFINE, all_hops * share)  48.5 us
    all_to_all x1, waiting for transfers between devices, shards(): lax.all_to_all(sending, 'tm', split_axis=3, concat_axis=0, tiled=True)  29.7 us
    unnamed x6, local copies, waits for them, and re-layouts  23.1 us
    transpose x1, local copies, waits for them, and re-layouts, shards(): col_filtered.transpose(1, 2, 0, 3).reshape(2 * NFINE, all_hops * share)  22.3 us
    reshape x1, local copies, waits for them, and re-layouts, shards(): sending = slots.transpose(2, 1, 3, 0, 4).reshape(HOPS_DEV, 2, NFINE, widest)  17.6 us
  transfers between devices with their start and end apart: 3, of which 3 were waited for; matrix products, arithmetic and copies ran while one was open for 8% of the time, Pallas kernels for 0%

commit v1 on v0

--- a/solution.py
+++ b/solution.py
@@ -10,6 +10,28 @@
 HOPS_DEV = 3
 MAXREQ = 4
 PAIR = 2
+
+
+def in_blocks(shard, dim, count):
+    before, after = (shard.shape[:dim], shard.shape[dim + 1 :])
+    return jnp.moveaxis(shard.reshape(*before, count, -1, *after), dim, 0)
+
+
+def laid_out(pieces, dim):
+    dims = list(pieces.shape[1:])
+    dims[dim] *= pieces.shape[0]
+    return jnp.moveaxis(pieces, 0, dim).reshape(dims)
+
+
+def pairwise_exchange(value, axis, split_dim, concat_dim):
+    size, index = (lax.axis_size(axis), lax.axis_index(axis))
+    blocks = in_blocks(value, split_dim, size)
+    outs = [blocks[index]]
+    for step in range(1, size):
+        sent = blocks[index ^ step]
+        outs.append(lax.ppermute(sent, axis, [(i, i ^ step) for i in range(size)]))
+    blocks = jnp.stack(outs)[index ^ jnp.arange(size)]
+    return laid_out(blocks, concat_dim)
 
 
 def build_table():
@@ -46,7 +68,7 @@
     outgoing = jnp.einsum(
         "dpb,xhkbc->dpxhkc", chooser, coarse_data, preferred_element_type=jnp.float32
     ).astype(jnp.bfloat16)
-    incoming = lax.all_to_all(outgoing, "chan", split_axis=0, concat_axis=0, tiled=True)
+    incoming = pairwise_exchange(outgoing, "chan", 0, 0)
     owner_ids = jnp.arange(owners, dtype=jnp.int32)
     row_pick = owner_ids == column
     my_block = jnp.sum(jnp.where(row_pick[:, None], req_block, 0), axis=0)

time: 611 us -> 712 us (1.17)
  local copies, waits for them, and re-layouts: 101 us -> 207 us
  matrix products: 133 us -> 124 us
  other arithmetic: 103 us -> 111 us
    all_to_all x1 -> x0, waiting for transfers between devices: 137 us -> none  [shards(): lax.all_to_all(outgoing, 'chan', split_axis=0, concat_axis=0, tiled=True)]
    ppermute x0 -> x3, waiting for transfers between devices: none -> 135 us  [pairwise_exchange(): outs.append(lax.ppermute(sent, axis, [(i, i ^ step) for i in range(size)]))]
    unnamed x6 -> x20, local copies, waits for them, and re-layouts: 23.1 us -> 75.3 us
    another operation x0 -> x1, local copies, waits for them, and re-layouts: none -> 38.8 us
    gather x0 -> x3, local copies, waits for them, and re-layouts: none -> 19 us  [pairwise_exchange(): blocks = jnp.stack(outs)[index ^ jnp.arange(size)]]
    convert_element_type x1 -> x0, local copies, waits for them, and re-layouts: 11.6 us -> none  [shards(): outgoing = jnp.einsum('dpb,xhkbc->dpxhkc', chooser, coarse_data, preferre...]
    dot_general x1, matrix products: 14.5 us -> 5.38 us  [shards(): jnp.einsum('qs,sxhkc->qxhkc', taker, arrived, preferred_element_type=jnp....]
    squeeze x0 -> x3, local copies, waits for them, and re-layouts: none -> 7.45 us  [pairwise_exchange(): sent = blocks[index ^ step]]
  transfers between devices with their start and end apart: 3 -> 5, of which waited for: 3 -> 5; matrix products, arithmetic and copies ran while one was open for 8% -> 8% of each run, Pallas kernels for 0% -> 0%
where the time goes in v1:
time: 712 us; the launch traced here: 705 us
  waiting for transfers between devices  243 us (34%)
  local copies, waits for them, and re-layouts  207 us (29%)
  matrix products  124 us (17%)
  other arithmetic  111 us (16%)
  starting transfers between devices  19.2 us (3%)
    ppermute x3, waiting for transfers between devices, pairwise_exchange(): outs.append(lax.ppermute(sent, axis, [(i, i ^ step) for i in range(size)]))  135 us
    dot_general x1, matrix products, shards(): jnp.dot(table, flat, precision=lax.Precision.HIGHEST, preferred_element_t...  112 us
    all_to_all x1, waiting for transfers between devices, shards(): lax.all_to_all(result, 'tm', split_axis=0, concat_axis=3, tiled=True)  77.8 us
    unnamed x20, local copies, waits for them, and re-layouts  75.3 us
    transpose x1, other arithmetic, shards(): col_filtered.transpose(1, 2, 0, 3).reshape(2 * NFINE, all_hops * share)  48.5 us
    another operation x1, local copies, waits for them, and re-layouts  38.8 us
    all_to_all x1, waiting for transfers between devices, shards(): lax.all_to_all(sending, 'tm', split_axis=3, concat_axis=0, tiled=True)  29.7 us
    transpose x1, local copies, waits for them, and re-layouts, shards(): col_filtered.transpose(1, 2, 0, 3).reshape(2 * NFINE, all_hops * share)  22.1 us
  transfers between devices with their start and end apart: 5, of which 5 were waited for; matrix products, arithmetic and copies ran while one was open for 8% of the time, Pallas kernels for 0%

profile of v1, /device:TPU:0, one launch (start us, length us, event | category | flops | bytes accessed | tf_op | source)
XLA Modules:
  0.0 705.3 jit_solution(7933105184799869549)
XLA Ops:
  2.4 7.8 %copy.67 = bf16[768,8,8,128]{3,2,1,0:T(8,128)(2,1)S(1)} copy(bf16[768,8,8,128]{3,1,2,0:T(8,128)(2,1)} %bitcast.101) | data formatting | bytes 25165824
  10.3 6.6 convolution_convert_fusion
  16.9 38.8 %constant_dynamic-slice_fusion.3 = (bf16[1,2,2,3,1024,128]{5,0,4,3,2,1:T(2,128)(2,1)}, bf16[1,2,2,3,1024,128]{5,0,4,3,2,1:T(2,128)(2,1)}, bf16[1,2,2,3,1024,128]...) fusion(bf16[4,2,2,3,1024,128]{5,0,4,3,2,1:T(4,128)(2,1)} %convolution_convert_fusion, s32[]{:T(128)S(6)} %select_n.84, ...), kind=kLoop, calls=%fused_computation.76 | loop fusion | bytes 25165840 | tf_op jit(solution)/shard_map/dynamic-slice
  55.8 3.5 copy.48
  60.9 3.5 copy.49
  70.8 59.5 %collective-permute-done = bf16[1,2,2,3,1024,128]{5,4,3,2,1,0:T(8,128)(2,1)S(1)} collective-permute-done((bf16[1,2,2,3,1024,128]{5,4,3,2,1,0:T(8,128)(2,1)S(1)}, bf16[1,2,2,3,1024,128]{5,4,3,2,1,0:T(8,128)(2,1)S(1)}, u32[]{:S(2)}, u32[]{:S(2)}) %collective-permute-start) | collective-permute-done | bytes 3145760 | tf_op jit(solution)/shard_map/ppermute | solution.py:32
  130.4 68.6 %collective-permute-done.1 = bf16[1,2,2,3,1024,128]{5,4,3,2,1,0:T(8,128)(2,1)S(1)} collective-permute-done((bf16[1,2,2,3,1024,128]{5,4,3,2,1,0:T(8,128)(2,1)S(1)}, bf16[1,2,2,3,1024,128]{5,4,3,2,1,0:T(8,128)(2,1)S(1)}, u32[]{:S(2)}, u32[]{:S(2)}) %collective-permute-start.1) | collective-permute-done | bytes 3145760 | tf_op jit(solution)/shard_map/ppermute | solution.py:32
  199.0 7.3 %collective-permute-done.2 = bf16[1,2,2,3,1024,128]{5,4,3,2,1,0:T(8,128)(2,1)S(1)} collective-permute-done((bf16[1,2,2,3,1024,128]{5,4,3,2,1,0:T(8,128)(2,1)S(1)}, bf16[1,2,2,3,1024,128]{5,4,3,2,1,0:T(8,128)(2,1)S(1)}, u32[]{:S(2)}, u32[]{:S(2)}) %collective-permute-start.2) | collective-permute-done | bytes 3145760 | tf_op jit(solution)/shard_map/ppermute | solution.py:32
  207.9 5.4 slice_bitcast_fusion.1
  213.3 6.8 gather_fusion
  220.1 6.8 gather_fusion.1
  226.9 6.0 pad_maximum_fusion.1
  232.9 51.6 %copy.51 = bf16[4,1,2,2,3,1024,128]{6,2,0,5,4,3,1:T(2,128)(2,1)S(1)} copy(bf16[4,1,2,2,3,1024,128]{6,5,4,3,2,0,1:T(8,128)(2,1)S(1)} %pad_maximum_fusion.1) | data formatting | bytes 25165824
  284.6 5.4 convert_bitcast_fusion.1
  289.9 17.6 %copy.65 = bf16[3,2,1024,4,128]{2,1,0,4,3:T(2,128)(2,1)} copy(bf16[3,2,1024,4,128]{4,3,2,0,1:T(4,128)(2,1)} %convert_bitcast_fusion.1) | data formatting | bytes 12582912 | tf_op jit(solution)/shard_map/reshape | solution.py:105
  307.6 8.8 %all-to-all-start = ((bf16[3,2,1024,512]{2,1,0,3:T(2,128)(2,1)}), bf16[3,2,1024,512]{2,1,0,3:T(2,128)(2,1)}, u32[]{:S(2)}, u32[]{:S(2)}) async-start(bf16[3,2,1024,512]{2,1,0,3:T(2,128)(2,1)} %bitcast.90), calls=%async_computation | async-start | bytes 12582912 | tf_op jit(solution)/shard_map/all_to_all | solution.py:106
  316.4 15.6 %fusion.12 = f32[1024,1024]{1,0:T(8,128)S(1)} fusion(), kind=kLoop, calls=%fused_computation.39 | loop fusion | flops 16777216 | bytes 4194304 | tf_op jit(solution)/shard_map/neg | solution.py:44
  332.0 16.6 %sine_multiply_fusion = (f32[1024,1024]{1,0:T(8,128)S(1)}, f32[1024,1024]{1,0:T(8,128)S(1)}) fusion(), kind=kLoop, calls=%fused_computation.33 | loop fusion | flops 16777216 | bytes 8388608 | tf_op jit(solution)/shard_map/div | solution.py:42
  348.6 15.7 %maximum_maximum_fusion = f32[2048,2048]{1,0:T(8,128)} fusion(f32[1024,1024]{1,0:T(8,128)S(1)} %get-tuple-element.34, f32[1024,1024]{1,0:T(8,128)S(1)} %fusion.12, f32[1024,1024]{1,0:T(8,128)S(1)} %get-tuple-element.33), kind=kLoop, calls=%fused_computation.2 | loop fusion | flops 12582912 | bytes 29360128 | tf_op jit(solution)/shard_map/concatenate | solution.py:45
  364.3 29.7 %all-to-all-done = bf16[3,2,1024,512]{2,1,0,3:T(2,128)(2,1)} async-done(((bf16[3,2,1024,512]{2,1,0,3:T(2,128)(2,1)}), bf16[3,2,1024,512]{2,1,0,3:T(2,128)(2,1)}, u32[]{:S(2)}, u32[]{:S(2)}) %all-to-all-start) | async-done | bytes 6291488 | tf_op jit(solution)/shard_map/all_to_all | solution.py:106
  394.0 4.8 copy.53
  398.8 3.4 copy.54
  402.2 48.5 %add_bitcast_fusion = f32[2,1024,96,16]{1,3,0,2:T(8,128)} fusion(bf16[96,2,1024,16]{2,3,1,0:T(8,128)(2,1)} %bitcast.97, f32[1024]{0:T(1024)S(1)} %bitcast.121, f32[1024]{0:T(1024)S(1)} %bitcast.122, f32[1024]{0:T(1024)S(1)} %bitcast.108, f32[1024]{0:T(1024)S(1)} %bitcast.109, f32[1024]{0:T(1024)S(1)} %bitcast.110, f32[1024]{0:T(1024)S(1)} %bitcast.111, ...), kind=kLoop, calls=%fused_computation.8 | loop fusion | flops 147849216 | bytes 18939904 | tf_op jit(solution)/shard_map/transpose | solution.py:115
  450.7 22.1 %copy.55 = f32[2,1024,96,16]{1,0,3,2:T(2,128)} copy(f32[2,1024,96,16]{1,3,0,2:T(8,128)} %add_bitcast_fusion) | data formatting | bytes 25165824 | tf_op jit(solution)/shard_map/transpose | solution.py:115
  472.8 15.3 %copy.68 = f32[192,8,2,1024]{3,1,2,0:T(8,128)} copy(f32[192,8,2,1024]{3,2,1,0:T(2,128)} %bitcast.89) | data formatting | bytes 25165824
  488.1 112.3 %convert_bitcast_fusion = bf16[96,2,1024,16]{2,0,3,1:T(8,128)(2,1)S(1)} fusion(f32[2,1024,2048,1]{2,1,3,0:T(8,128)} %bitcast.100, f32[96,16,2048]{2,1,0:T(8,128)} %bitcast.102), kind=kOutput, calls=%fused_computation.14 | convolution fusion | flops 77312557056 | bytes 35651584 | tf_op jit(solution)/shard_map/dot_general | solution.py:116
  600.4 6.2 copy.57
  606.6 5.0 all-to-all-start.1
  611.8 77.8 %all-to-all-done.1 = bf16[96,2,1024,16]{2,3,1,0:T(8,128)(2,1)} async-done(((bf16[96,2,1024,16]{2,3,1,0:T(8,128)(2,1)}), bf16[96,2,1024,16]{2,3,1,0:T(8,128)(2,1)}, u32[]{:S(2)}, u32[]{:S(2)}) %all-to-all-start.1) | async-done | bytes 6291488 | tf_op jit(solution)/shard_map/all_to_all | solution.py:120
  689.6 3.5 copy.58
  693.1 3.1 fusion.3
  696.2 8.6 %copy.59 = bf16[3,1,4,2,1024,128]{5,4,3,2,1,0:T(8,128)(2,1)} copy(bf16[3,1,4,2,1024,128]{4,5,2,3,0,1:T(8,128)(2,1)} %fusion.3) | data formatting | bytes 12582912 | tf_op jit(solution)/shard_map/broadcast_in_dim | solution.py:124
  (42 shorter events, 12.3 us)
Async XLA Ops:
  55.8 11.5 %slice-start.2 = ((s8[6291456]{0:T(1024)(128)(4,1)}), s8[4194304]{0:T(1024)(128)(4,1)S(1)}, s32[]{:S(2)}) async-start(s8[6291456]{0:T(1024)(128)(4,1)} %bitcast.93), calls=%async_computation.4 | async-start | bytes 8388608
  59.2 8.0 %slice-start.3 = ((s8[6291456]{0:T(1024)(128)(4,1)}), s8[2097152]{0:T(1024)(128)(4,1)S(1)}, s32[]{:S(2)}) async-start(s8[6291456]{0:T(1024)(128)(4,1)} %bitcast.93), calls=%async_computation.5 | async-start | bytes 4194304
  59.3 71.1 %collective-permute-start = (bf16[1,2,2,3,1024,128]{5,4,3,2,1,0:T(8,128)(2,1)S(1)}, bf16[1,2,2,3,1024,128]{5,4,3,2,1,0:T(8,128)(2,1)S(1)}, u32[]{:S(2)}, u32[]{:S(2)}) collective-permute-start(bf16[1,2,2,3,1024,128]{5,4,3,2,1,0:T(8,128)(2,1)S(1)} %copy.48), channel_id=1, source_target_pairs={{0,1},{1,0},{2,3},{3,2},{4,5},{5,4},{6,7},{7,6},{8,9},{9,8},{10,11... | collective-permute-start | bytes 9437192 | tf_op jit(solution)/shard_map/ppermute | solution.py:32
  60.9 7.8 %slice-start = ((s8[6291456]{0:T(1024)(128)(4,1)}), s8[4194304]{0:T(1024)(128)(4,1)S(1)}, s32[]{:S(2)}) async-start(s8[6291456]{0:T(1024)(128)(4,1)} %bitcast.91), calls=%async_computation.2 | async-start | bytes 8388608
  64.4 134.6 %collective-permute-start.1 = (bf16[1,2,2,3,1024,128]{5,4,3,2,1,0:T(8,128)(2,1)S(1)}, bf16[1,2,2,3,1024,128]{5,4,3,2,1,0:T(8,128)(2,1)S(1)}, u32[]{:S(2)}, u32[]{:S(2)}) collective-permute-start(bf16[1,2,2,3,1024,128]{5,4,3,2,1,0:T(8,128)(2,1)S(1)} %copy.49), channel_id=1, source_target_pairs={{0,2},{1,3},{2,0},{3,1},{4,6},{5,7},{6,4},{7,5},{8,10},{9,11},{10,... | collective-permute-start | bytes 9437192 | tf_op jit(solution)/shard_map/ppermute | solution.py:32
  67.2 1.6 slice-start.1
  67.7 1.6 copy-start.1
  67.7 138.5 %collective-permute-start.2 = (bf16[1,2,2,3,1024,128]{5,4,3,2,1,0:T(8,128)(2,1)S(1)}, bf16[1,2,2,3,1024,128]{5,4,3,2,1,0:T(8,128)(2,1)S(1)}, u32[]{:S(2)}, u32[]{:S(2)}) collective-permute-start(bf16[1,2,2,3,1024,128]{5,4,3,2,1,0:T(8,128)(2,1)S(1)} %copy.50), channel_id=1, source_target_pairs={{0,3},{1,2},{2,1},{3,0},{4,7},{5,6},{6,5},{7,4},{8,11},{9,10},{10,... | collective-permute-start | bytes 9437192 | tf_op jit(solution)/shard_map/ppermute | solution.py:32
  307.6 8.8 %copy-start = (f32[16,1024]{1,0:T(8,128)S(1)}, f32[16,1024]{1,0:T(8,128)}, u32[]{:S(2)}) copy-start(f32[16,1024]{1,0:T(8,128)} %param.7) | copy-start | bytes 196612
  307.6 86.5 %all-to-all-start = ((bf16[3,2,1024,512]{2,1,0,3:T(2,128)(2,1)}), bf16[3,2,1024,512]{2,1,0,3:T(2,128)(2,1)}, u32[]{:S(2)}, u32[]{:S(2)}) async-start(bf16[3,2,1024,512]{2,1,0,3:T(2,128)(2,1)} %bitcast.90), calls=%async_computation | async-start | bytes 12582912 | tf_op jit(solution)/shard_map/all_to_all | solution.py:106
  606.6 5.0 copy-start.2
  606.6 5.1 copy-start.3
  606.6 82.9 %all-to-all-start.1 = ((bf16[96,2,1024,16]{2,3,1,0:T(8,128)(2,1)}), bf16[96,2,1024,16]{2,3,1,0:T(8,128)(2,1)}, u32[]{:S(2)}, u32[]{:S(2)}) async-start(bf16[96,2,1024,16]{2,3,1,0:T(8,128)(2,1)} %copy.57), calls=%async_computation.1 | async-start | bytes 12582912 | tf_op jit(solution)/shard_map/all_to_all | solution.py:120
